TPU v7x, 32 devices: a whole 2x2x4 slice. The times are simulated.
32 devices in a mesh: grp: 2 (over x), ctx: 16 (over z, y, core).
Axes of the slice: x: 2, y: 2, z: 4, core: 2. Of those that a mesh axis runs over, the one named last changes fastest.
Arguments:
- queries: bfloat16 [2, 24, 64, 576], P('grp', None, 'ctx'), parts along dimension 0, may hold values from -40 to 40
- cache: bfloat16 [2, 8192, 576], P('grp', 'ctx'), parts along dimension 0, may hold values from -6 to 6
- draft_latent: bfloat16 [2, 24, 576], P('grp'), parts along dimension 0, may hold values from -9 to 9
- lengths: int32 [2], P('grp'), parts along dimension 0, may hold values from 4096 to 8192
- parents: int32 [2, 24], P('grp'), parts along dimension 0, may hold values from -1 to 22, as said below
- value_up: bfloat16 [64, 512, 128], P('ctx'), may hold values from -0.25 to 0.25
- out_proj: bfloat16 [8192, 7168], P('ctx'), may hold values from -0.09375 to 0.09375
Outputs:
- attended: bfloat16 [48, 7168], P('grp', 'ctx'), parts along dimension 0
There are 2 independent parts, one for each index of `grp`. A program takes and returns all parts, laid end to end along the dimension named above; an argument that names none is the same for every part. Nothing has to cross between parts.
Inputs may be any that keep to these rules, and one draw needn't show every extreme that they name: parents[r, 0] = -1 and 0 <= parents[r, i] < i for i >= 1.
All inputs are finite; a program needn't handle non-finite values.
Results may differ from a plain program's by a relative error of at most 0.007.
Values may be sent and summed in bfloat16 or wider, within the bound.
A program may use at most 64 MiB of HBM per device.

v0:
```python
import math

import jax
import jax.numpy as jnp
from jax import lax
from jax.sharding import PartitionSpec as P

yarn_factor = 1.0 + 0.1 * math.log(32.0)
score_scale = yarn_factor * yarn_factor / math.sqrt(192.0)
neg_fill = -1e30


def tree_reach(parents):
    drafts = parents.shape[1]
    order = jnp.arange(drafts, dtype=jnp.int32)
    adjacent = (parents[:, :, None] == order[None, None, :]).astype(jnp.float32)
    ident = jnp.broadcast_to(jnp.eye(drafts, dtype=jnp.float32), adjacent.shape)

    def extend(step, reach):
        grown = ident + jnp.einsum("rij,rjk->rik", adjacent, reach, precision=lax.Precision.HIGHEST)
        return jnp.minimum(grown, 1.0)

    return lax.fori_loop(0, drafts, extend, ident) > 0.5


def block_state(rows, keys, valid, latent_width):
    scores = (
        lax.dot_general(
            rows, keys, (((2,), (2,)), ((0,), (0,))), preferred_element_type=jnp.float32
        )
        * score_scale
    )
    masked = jnp.where(valid, scores, neg_fill)
    top = jnp.max(masked, axis=2)
    weights = jnp.where(valid, jnp.exp(masked - top[:, :, None]), 0.0).astype(jnp.bfloat16)
    numer = lax.dot_general(
        weights, keys, (((2,), (1,)), ((0,), (0,))), preferred_element_type=jnp.float32
    )
    total = jnp.sum(weights.astype(jnp.float32), axis=2)
    return (numer[:, :, :latent_width], top, total)


def join(first, second):
    best = jnp.maximum(first[1], second[1])
    factor_a = jnp.exp(first[1] - best)
    factor_b = jnp.exp(second[1] - best)
    return (
        first[0] * factor_a[..., None] + second[0] * factor_b[..., None],
        best,
        first[2] * factor_a + second[2] * factor_b,
    )


def on_device(queries, cache, draft_latent, lengths, parents, value_up, out_proj):
    requests, drafts, heads_here, width = queries.shape
    block_len = cache.shape[1]
    latent_width = value_up.shape[1]
    myself = lax.axis_index("ctx")
    positions = myself * block_len + jnp.arange(block_len, dtype=jnp.int32)
    live = (positions[None, :] < lengths[:, None])[:, None, :]
    own_rows = queries.reshape(requests, drafts * heads_here, width)
    every = lax.all_gather(queries, "ctx", axis=2, tiled=True)
    heads = every.shape[2]
    rows = every.reshape(requests, drafts * heads, width)
    numer, top, total = block_state(rows, cache, live, latent_width)
    numer = numer.reshape(1, requests, drafts, heads, latent_width)
    top = top.reshape(1, requests, drafts, heads)
    total = total.reshape(1, requests, drafts, heads)
    numers, tops, totals = (
        lax.all_to_all(numer, "ctx", split_axis=3, concat_axis=0, tiled=True),
        lax.all_to_all(top, "ctx", split_axis=3, concat_axis=0, tiled=True),
        lax.all_to_all(total, "ctx", split_axis=3, concat_axis=0, tiled=True),
    )
    best = jnp.max(tops, axis=0)
    factor = jnp.exp(tops - best[None])
    context = (
        jnp.sum(numers * factor[..., None], axis=0).reshape(
            requests, drafts * heads_here, latent_width
        ),
        best.reshape(requests, drafts * heads_here),
        jnp.sum(totals * factor, axis=0).reshape(requests, drafts * heads_here),
    )
    reach = tree_reach(parents)
    tree = jnp.repeat(reach, heads_here, axis=1)
    whole = join(context, block_state(own_rows, draft_latent, tree, latent_width))
    latent_out = (whole[0] / whole[2][..., None]).astype(jnp.bfloat16)
    latent_out = latent_out.reshape(requests, drafts, heads_here, latent_width)
    values = jnp.einsum(
        "rdhl,hlv->rdhv", latent_out, value_up, preferred_element_type=jnp.float32
    ).astype(jnp.bfloat16)
    flat = values.reshape(requests * drafts, heads_here * value_up.shape[2])
    partial_value = jnp.dot(flat, out_proj, preferred_element_type=jnp.float32)
    return lax.psum_scatter(partial_value, "ctx", scatter_dimension=1, tiled=True).astype(
        jnp.bfloat16
    )


def solution(mesh):
    in_specs = (
        P("grp", None, "ctx", None),
        P("grp", "ctx", None),
        P("grp", None, None),
        P("grp"),
        P("grp", None),
        P("ctx", None, None),
        P("ctx", None),
    )
    out_specs = P("grp", "ctx")
    return jax.shard_map(
        on_device, mesh=mesh, in_specs=in_specs, out_specs=out_specs, check_vma=False
    )
```

profile of v0, /device:TPU:0, one launch (start us, length us, event | category | flops | bytes accessed | tf_op | source)
XLA Modules:
  0.0 251.4 jit_solution(7607140488094526132)
XLA Ops:
  6.5 1.6 copy.40
  8.2 0.0 all-gather.2.cloned.1.call-update
  8.9 44.5 %all-gather.2.cloned.1.call-done = bf16[1,24,64,576]{3,1,0,2:T(8,128)(2,1)} async-done(((bf16[1,24,4,576]{3,1,0,2:T(8,128)(2,1)}), bf16[1,24,64,576]{3,1,0,2:T(8,128)(2,1)}) %all-gather.2.cloned.1.call-update) | async-done | bytes 1769488 | tf_op jit(solution)/shard_map/all_gather | solution.py:62
  53.4 1.9 copy.41
  55.3 1.5 fusion.29
  56.8 1.7 copy-done.1
  58.5 0.6 convert_reduce_fusion
  59.1 0.1 reshape.338
  59.1 0.7 copy.49
  59.8 3.5 %all-to-all-start.2 = ((f32[1,1,24,64]{2,1,0,3:T(1,128)}), f32[1,1,24,64]{2,1,0,3:T(1,128)S(1)}, u32[]{:S(2)}, u32[]{:S(2)}) async-start(f32[1,1,24,64]{2,1,0,3:T(1,128)} %copy.49), calls=%async_computation.2 | async-start | bytes 65536 | tf_op jit(solution)/shard_map/all_to_all | solution.py:72
  63.3 0.1 reshape.333
  63.4 0.7 copy.44
  64.1 5.9 %all-to-all-done.2 = f32[1,1,24,64]{2,1,0,3:T(1,128)S(1)} async-done(((f32[1,1,24,64]{2,1,0,3:T(1,128)}), f32[1,1,24,64]{2,1,0,3:T(1,128)S(1)}, u32[]{:S(2)}, u32[]{:S(2)}) %all-to-all-start.2) | async-done | bytes 6176 | tf_op jit(solution)/shard_map/all_to_all | solution.py:72
  69.9 3.5 %all-to-all-start.1 = ((f32[1,1,24,64]{2,1,0,3:T(1,128)}), f32[1,1,24,64]{2,1,0,3:T(1,128)S(1)}, u32[]{:S(2)}, u32[]{:S(2)}) async-start(f32[1,1,24,64]{2,1,0,3:T(1,128)} %copy.44), calls=%async_computation.1 | async-start | bytes 65536 | tf_op jit(solution)/shard_map/all_to_all | solution.py:71
  73.4 3.1 %convolution_bitcast_fusion.1 = f32[1,1536,576]{1,2,0:T(8,128)S(1)} fusion(bf16[1,512,576]{1,2,0:T(8,128)(2,1)S(1)} %copy-done, f32[1536,512]{0,1:T(8,128)} %copy-done.1, f32[1536]{0:T(1024)S(1)} %get-tuple-element.49, pred[512]{0:T(512)(128)(4,1)S(1)} %add_compare_fusion), kind=kOutput, calls=%fused_computation.12 | convolution fusion | flops 908328960 | bytes 7281152 | tf_op jit(solution)/shard_map/dot_general | solution.py:36
  76.5 1.9 slice.8
  78.4 3.6 %copy.42 = f32[1,1536,512]{2,1,0:T(8,128)} copy(f32[1,1536,512]{1,2,0:T(8,128)} %slice.8) | data formatting | bytes 6291456 | tf_op jit(solution)/shard_map/slice | solution.py:40
  82.0 5.4 %copy.43 = f32[1,1,24,64,512]{4,2,1,0,3:T(8,128)} copy(f32[1,1,24,64,512]{4,3,2,1,0:T(8,128)} %bitcast.82) | data formatting | bytes 6291456 | tf_op jit(solution)/shard_map/reshape | solution.py:66
  87.4 6.2 %all-to-all-start = ((f32[1,1,24,64,512]{4,2,1,0,3:T(8,128)}), f32[1,1,24,64,512]{4,2,1,0,3:T(8,128)}, u32[]{:S(2)}, u32[]{:S(2)}) async-start(f32[1,1,24,64,512]{4,2,1,0,3:T(8,128)} %copy.43), calls=%async_computation | async-start | bytes 6291456 | tf_op jit(solution)/shard_map/all_to_all | solution.py:70
  93.5 0.0 reduce-scatter.4.cloned.1.call-start
  93.6 0.1 reshape.336
  93.7 5.8 %while.11 = (s32[]{:T(128)}, f32[1,24,24]{2,1,0:T(8,128)S(1)}, s32[24]{0:T(128)S(1)}, s32[]{:T(128)}) while((s32[]{:T(128)}, f32[1,24,24]{2,1,0:T(8,128)S(1)}, s32[24]{0:T(128)S(1)}, s32[]{:T(128)}) %tuple.32), condition=%wide.region_4.5_spmd.clone, body=%wide.region_3.4_spmd.clone.sunk | while | flops 169346 | bytes 9365 | solution.py:23
  93.7 0.2 fusion.39
  94.0 0.2 fusion.39
  94.2 0.2 fusion.39
  94.4 0.2 fusion.39
  94.7 0.2 fusion.39
  94.9 0.2 fusion.39
  95.2 0.2 fusion.39
  95.4 0.2 fusion.39
  95.7 0.2 fusion.39
  95.9 0.2 fusion.39
  96.1 0.2 fusion.39
  96.4 0.2 fusion.39
  96.6 0.2 fusion.39
  96.9 0.2 fusion.39
  97.1 0.2 fusion.39
  97.3 0.2 fusion.39
  97.6 0.2 fusion.39
  97.8 0.2 fusion.39
  98.1 0.2 fusion.39
  98.3 0.2 fusion.39
  98.6 0.2 fusion.39
  98.8 0.2 fusion.39
  99.0 0.2 fusion.39
  99.3 0.2 fusion.39
  99.6 0.1 copy.47
  99.6 0.0 copy-done.4
  99.6 0.2 fusion.28
  99.9 0.2 convolution_bitcast_fusion.2
  100.1 0.1 copy.46
  100.3 0.1 copy.50
  100.3 0.1 reshape.339
  100.4 0.1 reshape.335
  100.6 52.2 %all-to-all-done = f32[1,1,24,64,512]{4,2,1,0,3:T(8,128)} async-done(((f32[1,1,24,64,512]{4,2,1,0,3:T(8,128)}), f32[1,1,24,64,512]{4,2,1,0,3:T(8,128)}, u32[]{:S(2)}, u32[]{:S(2)}) %all-to-all-start) | async-done | bytes 3145760 | tf_op jit(solution)/shard_map/all_to_all | solution.py:70
  152.8 2.2 multiply_reduce_fusion
  155.0 0.1 copy.45
  155.1 0.1 reshape.334
  155.2 0.1 fusion.17
  155.4 0.2 fusion.11
  155.6 7.8 %convolution_bitcast_fusion = f32[7168,24]{1,0:T(8,128)} fusion(bf16[512,7168]{1,0:T(8,128)(2,1)} %param.15, bf16[3,8,4,128]{3,2,1,0:T(4,128)(2,1)S(1)} %bitcast.90), kind=kOutput, calls=%fused_computation.11 | convolution fusion | flops 176160768 | bytes 8052736
  163.4 0.0 reduce-scatter.4.cloned.1.call-update
  163.5 79.5 %reduce-scatter.4.cloned.1.call-done = f32[448,24]{1,0:T(8,128)} async-done(((f32[7168,24]{1,0:T(8,128)}), f32[448,24]{1,0:T(8,128)}) %reduce-scatter.4.cloned.1.call-update) | async-done | bytes 43024
  243.0 1.6 copy.54
  (48 shorter events, 0.3 us)
Async XLA Ops:
  6.5 48.7 %copy-start = (bf16[1,512,576]{1,2,0:T(8,128)(2,1)S(1)}, bf16[1,512,576]{1,2,0:T(8,128)(2,1)}, u32[]{:S(2)}) copy-start(bf16[1,512,576]{1,2,0:T(8,128)(2,1)} %param.10) | copy-start | bytes 1769476
  6.5 46.9 %all-gather.2.cloned.1.call-start = ((), (), s32[]{:S(2)}) async-start(), calls=%async_computation.4 | async-start | bytes 2088960 | tf_op jit(solution)/shard_map/all_gather | solution.py:62
  56.8 1.7 copy-start.1
  59.8 10.1 %all-to-all-start.2 = ((f32[1,1,24,64]{2,1,0,3:T(1,128)}), f32[1,1,24,64]{2,1,0,3:T(1,128)S(1)}, u32[]{:S(2)}, u32[]{:S(2)}) async-start(f32[1,1,24,64]{2,1,0,3:T(1,128)} %copy.49), calls=%async_computation.2 | async-start | bytes 65536 | tf_op jit(solution)/shard_map/all_to_all | solution.py:72
  69.9 17.4 %all-to-all-start.1 = ((f32[1,1,24,64]{2,1,0,3:T(1,128)}), f32[1,1,24,64]{2,1,0,3:T(1,128)S(1)}, u32[]{:S(2)}, u32[]{:S(2)}) async-start(f32[1,1,24,64]{2,1,0,3:T(1,128)} %copy.44), calls=%async_computation.1 | async-start | bytes 65536 | tf_op jit(solution)/shard_map/all_to_all | solution.py:71
  87.3 6.2 %copy-start.3 = (bf16[1,24,4,576]{3,2,1,0:T(4,128)(2,1)S(1)}, bf16[1,24,4,576]{3,2,1,0:T(4,128)(2,1)}, u32[]{:S(2)}) copy-start(bf16[1,24,4,576]{3,2,1,0:T(4,128)(2,1)} %param.9) | copy-start | bytes 331780
  87.4 6.3 %copy-start.5 = (s32[1,24]{1,0:T(1,128)S(1)}, s32[1,24]{1,0:T(1,128)}, u32[]{:S(2)}) copy-start(s32[1,24]{1,0:T(1,128)} %param.13) | copy-start | bytes 292
  87.4 12.3 %copy-start.4 = (bf16[1,24,576]{2,1,0:T(8,128)(2,1)S(1)}, bf16[1,24,576]{2,1,0:T(8,128)(2,1)}, u32[]{:S(2)}) copy-start(bf16[1,24,576]{2,1,0:T(8,128)(2,1)} %param.11) | copy-start | bytes 82948
  87.4 65.5 %all-to-all-start = ((f32[1,1,24,64,512]{4,2,1,0,3:T(8,128)}), f32[1,1,24,64,512]{4,2,1,0,3:T(8,128)}, u32[]{:S(2)}, u32[]{:S(2)}) async-start(f32[1,1,24,64,512]{4,2,1,0,3:T(8,128)} %copy.43), calls=%async_computation | async-start | bytes 6291456 | tf_op jit(solution)/shard_map/all_to_all | solution.py:70
  93.5 149.4 %reduce-scatter.4.cloned.1.call-start = ((), (), s32[]{:S(2)}) async-start(), calls=%async_computation.5 | async-start | bytes 3899392
  93.7 61.7 %copy-start.2 = (bf16[4,512,128]{2,1,0:T(8,128)(2,1)S(1)}, bf16[4,512,128]{2,1,0:T(8,128)(2,1)}, u32[]{:S(2)}) copy-start(bf16[4,512,128]{2,1,0:T(8,128)(2,1)} %param.14) | copy-start | bytes 1572868
Sparse Core Ops, SparseCore 0:
  9.6 43.7 all-gather.1
  163.6 79.3 reduce-scatter.3
where the time goes:
time: 252 us; the launch traced here: 251 us
  waiting for transfers between devices  182 us (72%)
  local copies, waits for them, and re-layouts  20 us (8%)
  matrix products  18 us (7%)
  between operations  14.3 us (6%)
  starting transfers between devices  13.2 us (5%)
  other arithmetic  2.99 us (1%)
    unnamed x3, waiting for transfers between devices  79.5 us
    all_to_all x1, waiting for transfers between devices, on_device(): lax.all_to_all(numer, 'ctx', split_axis=3, concat_axis=0, tiled=True)  52.2 us
    all_gather x1, waiting for transfers between devices, on_device(): every = lax.all_gather(queries, 'ctx', axis=2, tiled=True)  44.5 us
    unnamed x1, matrix products  7.84 us
    all_to_all x1, starting transfers between devices, on_device(): lax.all_to_all(numer, 'ctx', split_axis=3, concat_axis=0, tiled=True)  6.16 us
    all_to_all x1, waiting for transfers between devices, on_device(): lax.all_to_all(total, 'ctx', split_axis=3, concat_axis=0, tiled=True)  5.86 us
    slice x2, local copies, waits for them, and re-layouts, block_state(): return (numer[:, :, :latent_width], top, total)  5.45 us
    reshape x1, local copies, waits for them, and re-layouts, on_device(): numer = numer.reshape(1, requests, drafts, heads, latent_width)  5.38 us
  transfers between devices with their start and end apart: 5, of which 4 were waited for; matrix products, arithmetic and copies ran while one was open for 8% of the time, Pallas kernels for 0%

commit v1 on v0

v1 whole, which is shorter than its diff:
```python
import functools
import math

import jax
import jax.numpy as jnp
from jax import lax
from jax.experimental import pallas as pl
from jax.experimental.pallas import tpu as pltpu
from jax.sharding import PartitionSpec as P

yarn_factor = 1.0 + 0.1 * math.log(32.0)
score_scale = yarn_factor * yarn_factor / math.sqrt(192.0)
neg_fill = -1e30
MESH = pl.DeviceIdType.MESH
pieces = 4


def dot_nt(a, b):
    return lax.dot_general(a, b, (((1,), (1,)), ((), ())), preferred_element_type=jnp.float32)


def dot_nn(a, b):
    return lax.dot_general(a, b, (((1,), (0,)), ((), ())), preferred_element_type=jnp.float32)


def kernel(
    n, quad, heads, drafts, latent, width, vdim,
    q_hbm, cache_hbm, draft_hbm, lengths_ref, parents_ref, up_hbm, proj_hbm,
    out_ref,
    qbuf, kv, draft, up, proj, acc, state_out, state_in, stat_out, stat_in, share_out, share_in,
    load_sem, own_send, own_recv, near_send, near_recv, relay_send, relay_recv,
    q_send, q_recv, st_send, st_recv, stat_send, stat_recv, share_send, share_recv,
):
    me = lax.axis_index("ctx")
    depth = n // quad
    rows = drafts * heads
    block = cache_hbm.shape[0]
    piece = block // pieces
    z = lax.div(me, quad)
    q = lax.rem(me, quad)
    core = lax.rem(q, 2)
    other = q + 1 - 2 * core
    partner = z * quad + other
    two_chips = quad > 2
    near_q = lax.rem(q + 2, quad)
    near = z * quad + near_q
    near_other_q = near_q + 1 - 2 * core

    def load(src, dst, i):
        copy = pltpu.make_async_copy(src, dst, load_sem.at[i])
        copy.start()
        return copy

    get_kv = load(cache_hbm, kv.at[0], 0)
    get_q = load(q_hbm, qbuf.at[0], 1)
    get_draft = load(draft_hbm, draft, 2)
    get_up = load(up_hbm, up, 3)
    get_proj = load(proj_hbm, proj, 4)

    barrier = pltpu.get_barrier_semaphore()
    for o in range(1, n):
        pl.semaphore_signal(
            barrier, inc=1, device_id={"ctx": lax.rem(me + o, n)}, device_id_type=MESH
        )
    pl.semaphore_wait(barrier, n - 1)

    def remote(src, dst, send, recv, device):
        copy = pltpu.make_async_remote_copy(
            src_ref=src, dst_ref=dst, send_sem=send, recv_sem=recv,
            device_id={"ctx": device}, device_id_type=MESH,
        )
        copy.start()
        return copy

    sent = []
    near_copies = []
    if two_chips:
        for c in range(pieces):
            part = pl.ds(c * piece, piece)
            near_copies.append(remote(
                cache_hbm.at[part], kv.at[2, part], near_send.at[c], near_recv.at[c], near
            ))
    q_copies = []
    for o in range(1, depth):
        dest = lax.rem(z + o, depth) * quad + q
        q_copies.append(remote(q_hbm, qbuf.at[o], q_send.at[o], q_recv.at[o], dest))
    own = remote(cache_hbm, kv.at[1], own_send, own_recv, partner)

    row_id = lax.broadcasted_iota(jnp.int32, (drafts, drafts), 0)
    col_id = lax.broadcasted_iota(jnp.int32, (drafts, drafts), 1)
    eye = jnp.where(row_id == col_id, 1.0, 0.0)
    reach = jnp.where(row_id == jnp.broadcast_to(parents_ref[...], (drafts, drafts)), 1.0, eye)
    for _ in range(max(1, math.ceil(math.log2(drafts)))):
        low = reach.astype(jnp.bfloat16)
        reach = jnp.minimum(dot_nn(low, low), 1.0)
    reach = lax.dot_general(
        reach.astype(jnp.bfloat16), eye.astype(jnp.bfloat16), (((0,), (0,)), ((), ())),
        preferred_element_type=jnp.float32,
    )
    tree = jnp.concatenate([reach] * heads, axis=0) > 0.5
    get_q.wait()
    get_draft.wait()
    keys = draft[...]
    d_score = jnp.where(tree, dot_nt(qbuf[0], keys) * score_scale, neg_fill)
    d_top = jnp.max(d_score, axis=1, keepdims=True)
    d_weight = jnp.where(tree, jnp.exp(d_score - d_top), 0.0).astype(jnp.bfloat16)
    d_total = jnp.sum(d_weight.astype(jnp.float32), axis=1, keepdims=True)
    d_numer = dot_nn(d_weight, keys[:, :latent])

    relays = []

    def relay(c):
        if two_chips:
            part = pl.ds(c * piece, piece)
            near_copies[c].wait_recv()
            relays.append(remote(
                kv.at[2, part], kv.at[3, part], relay_send.at[c], relay_recv.at[c], partner
            ))

    limit = lengths_ref[0]
    joined = rows % 8 == 0 and depth <= 8
    groups = [(0, depth)] if joined else [(o, 1) for o in range(depth)]
    tops = {}
    totals = {}

    def attend(slot, owner_q):
        first = (z * quad + owner_q) * block
        live = (first + lax.broadcasted_iota(jnp.int32, (1, block), 1)) < limit
        for base, count in groups:
            span = count * rows
            query = qbuf[pl.ds(base, count)].reshape(span, width)
            scores = jnp.where(live, dot_nt(query, kv[slot]) * score_scale, neg_fill)
            top = jnp.max(scores, axis=1, keepdims=True)
            place = pl.ds(base * rows, span)
            if base in tops:
                best = jnp.maximum(tops[base], top)
                decay = jnp.exp(tops[base] - best)
            else:
                best = top
            weights = jnp.where(live, jnp.exp(scores - best), 0.0).astype(jnp.bfloat16)
            total = jnp.sum(weights.astype(jnp.float32), axis=1, keepdims=True)
            numer = dot_nn(weights, kv[slot, :, pl.ds(0, latent)])
            if base in tops:
                totals[base] = totals[base] * decay + total
                acc[place] = acc[place] * decay + numer
            else:
                totals[base] = total
                acc[place] = numer
            tops[base] = best

    for c in range(0, pieces - 2):
        relay(c)
    for copy in q_copies:
        copy.wait_recv()
    get_kv.wait()
    attend(0, q)
    own.wait_recv()
    relay(pieces - 2)
    attend(1, other)
    relay(pieces - 1)
    if two_chips:
        attend(2, near_q)
        for copy in relays:
            copy.wait_recv()
        attend(3, near_other_q)

    lane = lax.broadcasted_iota(jnp.int32, (rows, 128), 1)
    fill = jnp.zeros((128 - rows, 128), jnp.float32)
    state_copies = []
    stat_copies = []

    def stats_of(o):
        base, count = next(g for g in groups if g[0] <= o < g[0] + g[1])
        at = (o - base) * rows
        return tops[base][at : at + rows], totals[base][at : at + rows]

    for o in range(1, depth):
        top, total = stats_of(o)
        state_out[o] = acc[pl.ds(o * rows, rows)].astype(jnp.bfloat16)
        column = jnp.where(lane == 0, top, jnp.where(lane == 1, total, 0.0))
        stat_out[o] = jnp.concatenate([column, fill], axis=0).T[:8]
        back = depth - o
        dest = lax.rem(z + back, depth) * quad + q
        state_copies.append(remote(
            state_out.at[o], state_in.at[back], st_send.at[o], st_recv.at[back], dest
        ))
        stat_copies.append(remote(
            stat_out.at[o], stat_in.at[back], stat_send.at[o], stat_recv.at[back], dest
        ))

    def arrived(buf, send, recv, slot):
        return pltpu.make_async_remote_copy(
            src_ref=buf.at[slot], dst_ref=buf.at[slot], send_sem=send.at[slot],
            recv_sem=recv.at[slot], device_id={"ctx": partner}, device_id_type=MESH,
        )

    top0, total0 = stats_of(0)
    for s in range(1, depth):
        arrived(stat_in, stat_send, stat_recv, s).wait_recv()
    shown = jnp.concatenate(
        [stat_in[s] for s in range(1, depth)]
        + [jnp.zeros((-(depth - 1) * 8 % 128, 128), jnp.float32)], axis=0
    ).T
    their_top = [None] + [shown[:rows, 8 * s : 8 * s + 1] for s in range(depth - 1)]
    their_total = [None] + [shown[:rows, 8 * s + 1 : 8 * s + 2] for s in range(depth - 1)]
    best = jnp.maximum(top0, d_top)
    for s in range(1, depth):
        best = jnp.maximum(best, their_top[s])
    f0, fd = jnp.exp(top0 - best), jnp.exp(d_top - best)
    total = total0 * f0 + d_total * fd
    numer = acc[pl.ds(0, rows)] * f0 + d_numer * fd
    for s in range(1, depth):
        factor = jnp.exp(their_top[s] - best)
        total = total + their_total[s] * factor
        arrived(state_in, st_send, st_recv, s).wait_recv()
        numer = numer + state_in[s].astype(jnp.float32) * factor
    latent_out = (numer / total).astype(jnp.bfloat16).astype(jnp.float32)

    get_up.wait()
    values = [
        dot_nn(
            latent_out[h * drafts : (h + 1) * drafts].astype(jnp.bfloat16), up[h]
        ).astype(jnp.bfloat16)
        for h in range(heads)
    ]
    flat = jnp.concatenate(values, axis=1) if heads > 1 else values[0]

    cols = share_in.shape[2]
    per = 128 // math.gcd(cols, 128)
    n_groups = n // per
    mine, seat = lax.div(me, per), lax.rem(me, per)
    get_proj.wait()
    share_copies = []
    for j in list(range(1, n_groups)) + [0]:
        target = lax.rem(mine + j, n_groups)
        start = pl.multiple_of(target * (per * cols), 128)
        product = dot_nn(flat, proj[:, pl.ds(start, per * cols)])
        for t in range(per):
            shifted = product if t == 0 else pltpu.roll(product, per * cols - t * cols, 1)
            share_out[j * per + t] = shifted[:, :cols].astype(jnp.bfloat16)
        if j > 0:
            for t in range(per):
                slot = j * per + seat
                share_copies.append(remote(
                    share_out.at[j * per + t], share_in.at[slot],
                    share_send.at[j * per + t], share_recv.at[slot], target * per + t,
                ))
        else:
            for s in range(1, per):
                t = lax.rem(seat + s, per)
                share_copies.append(remote(
                    share_out.at[t], share_in.at[s],
                    share_send.at[s], share_recv.at[s], mine * per + t,
                ))
    result = share_out[seat].astype(jnp.float32)
    for s in list(range(1, per)) + list(range(per, n)):
        arrived(share_in, share_send, share_recv, s).wait_recv()
        result = result + share_in[s].astype(jnp.float32)
    out_ref[...] = result.astype(jnp.bfloat16)

    own.wait_send()
    for copy in near_copies + relays + q_copies + state_copies + stat_copies + share_copies:
        copy.wait_send()


def on_device(quad, n, queries, cache, draft_latent, lengths, parents, value_up, out_proj):
    _, drafts, heads, width = queries.shape
    block = cache.shape[1]
    latent, vdim = value_up.shape[1:]
    depth = n // quad
    rows = drafts * heads
    model = out_proj.shape[1]
    cols = model // n
    ordered = jnp.swapaxes(queries[0], 0, 1).reshape(rows, width)
    anywhere = pl.BlockSpec(memory_space=pl.ANY)
    in_vmem = pl.BlockSpec(memory_space=pltpu.VMEM)
    in_smem = pl.BlockSpec(memory_space=pltpu.SMEM)
    dma = pltpu.SemaphoreType.DMA
    bf16 = jnp.bfloat16
    return pl.pallas_call(
        functools.partial(kernel, n, quad, heads, drafts, latent, width, vdim),
        out_shape=jax.ShapeDtypeStruct((drafts, cols), bf16),
        in_specs=[anywhere, anywhere, anywhere, in_smem, in_vmem, anywhere, anywhere],
        out_specs=in_vmem,
        scratch_shapes=[
            pltpu.VMEM((depth, rows, width), bf16),
            pltpu.VMEM((quad, block, width), bf16),
            pltpu.VMEM((drafts, width), bf16),
            pltpu.VMEM((heads, latent, vdim), bf16),
            pltpu.VMEM((heads * vdim, model), bf16),
            pltpu.VMEM((depth * rows, latent), jnp.float32),
            pltpu.VMEM((depth, rows, latent), bf16),
            pltpu.VMEM((depth, rows, latent), bf16),
            pltpu.VMEM((depth, 8, 128), jnp.float32),
            pltpu.VMEM((depth, 8, 128), jnp.float32),
            pltpu.VMEM((n, drafts, cols), bf16),
            pltpu.VMEM((n, drafts, cols), bf16),
            dma((5,)),
            dma, dma,
            dma((pieces,)), dma((pieces,)),
            dma((pieces,)), dma((pieces,)),
            dma((depth,)), dma((depth,)),
            dma((depth,)), dma((depth,)),
            dma((depth,)), dma((depth,)),
            dma((n,)), dma((n,)),
        ],
        compiler_params=pltpu.CompilerParams(
            collective_id=0, has_side_effects=True, vmem_limit_bytes=56 * 1024 * 1024
        ),
    )(ordered, cache[0], draft_latent[0], lengths, parents, value_up, out_proj)


def quad_of(mesh):
    line = mesh.devices.reshape(mesh.shape["grp"], mesh.shape["ctx"])[0]
    depth = len({d.coords[2] for d in line})
    return len(line) // depth


def solution(mesh):
    in_specs = (
        P("grp", None, "ctx", None),
        P("grp", "ctx", None),
        P("grp", None, None),
        P("grp"),
        P("grp", None),
        P("ctx", None, None),
        P("ctx", None),
    )
    out_specs = P("grp", "ctx")
    return jax.shard_map(
        functools.partial(on_device, quad_of(mesh), mesh.shape["ctx"]),
        mesh=mesh, in_specs=in_specs, out_specs=out_specs, check_vma=False,
    )
```

time: 252 us -> 50.9 us (0.20)
  waiting for transfers between devices: 182 us -> 0 us
  Pallas kernels: 0 us -> 44.6 us
  matrix products: 18 us -> 0 us
  local copies, waits for them, and re-layouts: 20 us -> 5.04 us
  between operations: 14.3 us -> 0.66 us
  starting transfers between devices: 13.2 us -> 0 us
  other arithmetic: 2.99 us -> 0 us
    unnamed x3 -> x0, waiting for transfers between devices: 79.5 us -> none
    all_to_all x3 -> x0, waiting for transfers between devices: 58.1 us -> none  [the longest x1 52.2 us: on_device(): lax.all_to_all(numer, 'ctx', split_axis=3, concat_axis=0, tiled=True)]
    pallas_call x0 -> x1, Pallas kernels: none -> 44.6 us  [on_device(): pl.pallas_call(functools.partial(kernel, n, quad, heads, drafts, latent,...]
    all_gather x1 -> x0, waiting for transfers between devices: 44.5 us -> none  [on_device(): every = lax.all_gather(queries, 'ctx', axis=2, tiled=True)]
    all_to_all x3 -> x0, starting transfers between devices: 13.1 us -> none  [the longest x1 6.16 us: on_device(): lax.all_to_all(numer, 'ctx', split_axis=3, concat_axis=0, tiled=True)]
    dot_general x29 -> x0, matrix products: 10.2 us -> none  [the longest x24 4.96 us: extend(): jnp.einsum('rij,rjk->rik', adjacent, reach, precision=lax.Precision.HIGHEST)]
    unnamed x1 -> x0, matrix products: 7.84 us -> none
    reshape x8 -> x0, local copies, waits for them, and re-layouts: 7.15 us -> none  [the longest x1 5.38 us: on_device(): numer = numer.reshape(1, requests, drafts, heads, latent_width)]
  transfers between devices with their start and end apart: 5 -> 0, of which waited for: 4 -> 0; matrix products, arithmetic and copies ran while one was open for 8% -> 0% of each run, Pallas kernels for 0% -> 0%
where the time goes in v1:
time: 50.9 us; the launch traced here: 50.3 us
  Pallas kernels  44.6 us (88%)
  local copies, waits for them, and re-layouts  5.04 us (10%)
  between operations  0.66 us (1%)
    pallas_call x1, Pallas kernels, on_device(): pl.pallas_call(functools.partial(kernel, n, quad, heads, drafts, latent,...  44.6 us
    unnamed x2, local copies, waits for them, and re-layouts  3.49 us
    transpose x1, local copies, waits for them, and re-layouts, on_device(): ordered = jnp.swapaxes(queries[0], 0, 1).reshape(rows, width)  1.55 us

profile of v1, /device:TPU:0, one launch (start us, length us, event | category | flops | bytes accessed | tf_op | source)
XLA Modules:
  0.0 50.3 jit_solution(7637736412906854186)
XLA Ops:
  0.7 1.6 %copy.8 = bf16[4,24,576]{2,1,0:T(8,128)(2,1)} copy(bf16[4,24,576]{2,0,1:T(4,128)(2,1)} %bitcast.8) | data formatting | bytes 221184 | tf_op jit(solution)/shard_map/transpose | solution.py:274
  2.2 2.1 %copy.9 = bf16[1,512,576]{2,1,0:T(8,128)(2,1)} copy(bf16[1,512,576]{1,2,0:T(8,128)(2,1)} %param.8) | data formatting | bytes 1179648 | tf_op args[1]
  4.3 44.6 %shard_map.73 = bf16[24,448]{1,0:T(8,128)(2,1)} custom-call(bf16[96,576]{1,0:T(8,128)(2,1)} %bitcast.7, bf16[512,576]{1,0:T(8,128)(2,1)} %bitcast.6, bf16[24,576]{1,0:T(8,128)(2,1)} %bitcast.9, s32[1]{0:T(128)S(6)} %copy.11.lengths_ref, s32[1,24]{1,0:T(1,128)} %parents_ref.1, bf16[4,512,128]{2,1,0:T(8,128)(2,1)} %up_hbm.1, bf16[512,7168]{1,0:T(8,128)(2,1)} %proj_hbm.1), custom_call_target="tpu_custom_call" | custom-call | tf_op jit(solution)/shard_map/pallas_call | solution.py:280
  49.0 1.3 %copy.12 = bf16[24,448]{1,0:T(8,128)(2,1)} copy(bf16[24,448]{1,0:T(8,128)(2,1)} %shard_map.73) | data formatting | bytes 43008

commit v2 on v1

--- a/solution.py
+++ b/solution.py
@@ -27,15 +27,15 @@
     n, quad, heads, drafts, latent, width, vdim,
     q_hbm, cache_hbm, draft_hbm, lengths_ref, parents_ref, up_hbm, proj_hbm,
     out_ref,
-    qbuf, kv, draft, up, proj, acc, state_out, state_in, stat_out, stat_in, share_out, share_in,
+    qraw, qsplit, qbuf, kv, draft, up, proj, acc, state_out, state_in, stat_out, stat_in, share_out, share_in,
     load_sem, own_send, own_recv, near_send, near_recv, relay_send, relay_recv,
     q_send, q_recv, st_send, st_recv, stat_send, stat_recv, share_send, share_recv,
 ):
     me = lax.axis_index("ctx")
     depth = n // quad
     rows = drafts * heads
-    block = cache_hbm.shape[0]
-    piece = block // pieces
+    block = cache_hbm.shape[1]
+    piece = width // pieces
     z = lax.div(me, quad)
     q = lax.rem(me, quad)
     core = lax.rem(q, 2)
@@ -52,7 +52,7 @@
         return copy
 
     get_kv = load(cache_hbm, kv.at[0], 0)
-    get_q = load(q_hbm, qbuf.at[0], 1)
+    get_q = load(q_hbm, qraw, 1)
     get_draft = load(draft_hbm, draft, 2)
     get_up = load(up_hbm, up, 3)
     get_proj = load(proj_hbm, proj, 4)
@@ -62,6 +62,21 @@
         pl.semaphore_signal(
             barrier, inc=1, device_id={"ctx": lax.rem(me + o, n)}, device_id_type=MESH
         )
+
+    get_q.wait()
+    for i in range(drafts):
+        line = qraw[i].astype(jnp.float32)
+        for c in range(0, width, 128):
+            lanes = min(128, width - c)
+            qsplit[c // 128, pl.ds(i * heads, heads), pl.ds(0, lanes)] = line[:, c : c + lanes]
+    for h in range(heads):
+        for c in range(0, width, 128):
+            lanes = min(128, width - c)
+            turned = qsplit[c // 128, pl.ds(h, drafts, stride=heads), :]
+            qbuf[0, pl.ds(h * drafts, drafts), pl.ds(c, lanes)] = turned[:, :lanes].astype(
+                jnp.bfloat16
+            )
+
     pl.semaphore_wait(barrier, n - 1)
 
     def remote(src, dst, send, recv, device):
@@ -83,7 +98,7 @@
     q_copies = []
     for o in range(1, depth):
         dest = lax.rem(z + o, depth) * quad + q
-        q_copies.append(remote(q_hbm, qbuf.at[o], q_send.at[o], q_recv.at[o], dest))
+        q_copies.append(remote(qbuf.at[0], qbuf.at[o], q_send.at[o], q_recv.at[o], dest))
     own = remote(cache_hbm, kv.at[1], own_send, own_recv, partner)
 
     row_id = lax.broadcasted_iota(jnp.int32, (drafts, drafts), 0)
@@ -98,7 +113,6 @@
         preferred_element_type=jnp.float32,
     )
     tree = jnp.concatenate([reach] * heads, axis=0) > 0.5
-    get_q.wait()
     get_draft.wait()
     keys = draft[...]
     d_score = jnp.where(tree, dot_nt(qbuf[0], keys) * score_scale, neg_fill)
@@ -129,7 +143,7 @@
         for base, count in groups:
             span = count * rows
             query = qbuf[pl.ds(base, count)].reshape(span, width)
-            scores = jnp.where(live, dot_nt(query, kv[slot]) * score_scale, neg_fill)
+            scores = jnp.where(live, dot_nn(query, kv[slot]) * score_scale, neg_fill)
             top = jnp.max(scores, axis=1, keepdims=True)
             place = pl.ds(base * rows, span)
             if base in tops:
@@ -139,7 +153,7 @@
                 best = top
             weights = jnp.where(live, jnp.exp(scores - best), 0.0).astype(jnp.bfloat16)
             total = jnp.sum(weights.astype(jnp.float32), axis=1, keepdims=True)
-            numer = dot_nn(weights, kv[slot, :, pl.ds(0, latent)])
+            numer = dot_nt(weights, kv[slot, pl.ds(0, latent), :])
             if base in tops:
                 totals[base] = totals[base] * decay + total
                 acc[place] = acc[place] * decay + numer
@@ -271,7 +285,6 @@
     rows = drafts * heads
     model = out_proj.shape[1]
     cols = model // n
-    ordered = jnp.swapaxes(queries[0], 0, 1).reshape(rows, width)
     anywhere = pl.BlockSpec(memory_space=pl.ANY)
     in_vmem = pl.BlockSpec(memory_space=pltpu.VMEM)
     in_smem = pl.BlockSpec(memory_space=pltpu.SMEM)
@@ -283,8 +296,10 @@
         in_specs=[anywhere, anywhere, anywhere, in_smem, in_vmem, anywhere, anywhere],
         out_specs=in_vmem,
         scratch_shapes=[
+            pltpu.VMEM((drafts, heads, width), bf16),
+            pltpu.VMEM((pl.cdiv(width, 128), rows, 128), jnp.float32),
             pltpu.VMEM((depth, rows, width), bf16),
-            pltpu.VMEM((quad, block, width), bf16),
+            pltpu.VMEM((quad, width, block), bf16),
             pltpu.VMEM((drafts, width), bf16),
             pltpu.VMEM((heads, latent, vdim), bf16),
             pltpu.VMEM((heads * vdim, model), bf16),
@@ -307,7 +322,7 @@
         compiler_params=pltpu.CompilerParams(
             collective_id=0, has_side_effects=True, vmem_limit_bytes=56 * 1024 * 1024
         ),
-    )(ordered, cache[0], draft_latent[0], lengths, parents, value_up, out_proj)
+    )(queries[0], cache[0].T, draft_latent[0], lengths, parents, value_up, out_proj)
 
 
 def quad_of(mesh):

time: 50.9 us -> 45.7 us (0.90)
  local copies, waits for them, and re-layouts: 5.04 us -> 1.35 us
  Pallas kernels: 44.6 us -> 43.2 us
    unnamed x2 -> x1, local copies, waits for them, and re-layouts: 3.49 us -> 1.35 us
    transpose x1 -> x0, local copies, waits for them, and re-layouts: 1.55 us -> none  [on_device(): ordered = jnp.swapaxes(queries[0], 0, 1).reshape(rows, width)]
    pallas_call x1, Pallas kernels: 44.6 us -> 43.2 us  [on_device(): pl.pallas_call(functools.partial(kernel, n, quad, heads, drafts, latent,...]
where the time goes in v2:
time: 45.7 us; the launch traced here: 45.2 us
  Pallas kernels  43.2 us (95%)
  local copies, waits for them, and re-layouts  1.35 us (3%)
  between operations  0.66 us (1%)
    pallas_call x1, Pallas kernels, on_device(): pl.pallas_call(functools.partial(kernel, n, quad, heads, drafts, latent,...  43.2 us
    unnamed x1, local copies, waits for them, and re-layouts  1.35 us

profile of v2, /device:TPU:0, one launch (start us, length us, event | category | flops | bytes accessed | tf_op | source)
XLA Modules:
  0.0 45.2 jit_solution(5638105999492181186)
XLA Ops:
  0.7 43.2 %shard_map.73 = bf16[24,448]{1,0:T(8,128)(2,1)} custom-call(bf16[24,4,576]{2,1,0:T(4,128)(2,1)} %bitcast.6, bf16[576,512]{1,0:T(8,128)(2,1)} %bitcast.5, bf16[24,576]{1,0:T(8,128)(2,1)} %bitcast.7, s32[1]{0:T(128)S(6)} %copy.9.lengths_ref, s32[1,24]{1,0:T(1,128)} %parents_ref.1, bf16[4,512,128]{2,1,0:T(8,128)(2,1)} %up_hbm.1, bf16[512,7168]{1,0:T(8,128)(2,1)} %proj_hbm.1), custom_call_target="tpu_custom_call" | custom-call | tf_op jit(solution)/shard_map/pallas_call | solution.py:293
  43.9 1.3 %copy.10 = bf16[24,448]{1,0:T(8,128)(2,1)} copy(bf16[24,448]{1,0:T(8,128)(2,1)} %shard_map.73) | data formatting | bytes 43008

commit v3 on v2

--- a/solution.py
+++ b/solution.py
@@ -27,9 +27,11 @@
     n, quad, heads, drafts, latent, width, vdim,
     q_hbm, cache_hbm, draft_hbm, lengths_ref, parents_ref, up_hbm, proj_hbm,
     out_ref,
-    qraw, qsplit, qbuf, kv, draft, up, proj, acc, state_out, state_in, stat_out, stat_in, share_out, share_in,
-    load_sem, own_send, own_recv, near_send, near_recv, relay_send, relay_recv,
-    q_send, q_recv, st_send, st_recv, stat_send, stat_recv, share_send, share_recv,
+    qraw, qsplit, qbuf, kv, draft, up, proj, acc, state_out, state_in, stat_out, stat_in,
+    share, kept, pair_out, pair_in, share_out, share_in,
+    from_up, from_down, load_sem, own_send, own_recv, near_send, near_recv, relay_send, relay_recv,
+    q_send, q_recv, st_send, st_recv, stat_send, stat_recv,
+    pair_send, pair_recv, share_send, share_recv,
 ):
     me = lax.axis_index("ctx")
     depth = n // quad
@@ -58,10 +60,22 @@
     get_proj = load(proj_hbm, proj, 4)
 
     barrier = pltpu.get_barrier_semaphore()
-    for o in range(1, n):
-        pl.semaphore_signal(
-            barrier, inc=1, device_id={"ctx": lax.rem(me + o, n)}, device_id_type=MESH
-        )
+
+    def signal(sem, device):
+        pl.semaphore_signal(sem, inc=1, device_id={"ctx": device}, device_id_type=MESH)
+
+    last = depth - 1
+    signal(barrier, partner)
+    if two_chips:
+        signal(barrier, near)
+
+    @pl.when(z < last)
+    def _():
+        signal(barrier, me + quad)
+
+    @pl.when(z > 0)
+    def _():
+        signal(barrier, me - quad)
 
     get_q.wait()
     for i in range(drafts):
@@ -77,7 +91,8 @@
                 jnp.bfloat16
             )
 
-    pl.semaphore_wait(barrier, n - 1)
+    ends = lax.div(z + last, depth) + lax.div(last - z + last, depth)
+    pl.semaphore_wait(barrier, ends + (2 if two_chips else 1))
 
     def remote(src, dst, send, recv, device):
         copy = pltpu.make_async_remote_copy(
@@ -95,11 +110,29 @@
             near_copies.append(remote(
                 cache_hbm.at[part], kv.at[2, part], near_send.at[c], near_recv.at[c], near
             ))
+    own = remote(cache_hbm, kv.at[1], own_send, own_recv, partner)
+
+    for r in range(1, last):
+        @pl.when((z >= 1) & (z + r <= last))
+        def _():
+            signal(from_up.at[r], me - quad)
+
+        @pl.when((z < last) & (z >= r))
+        def _():
+            signal(from_down.at[r], me + quad)
+
+        @pl.when(z + 1 + r <= last)
+        def _():
+            pl.semaphore_wait(from_up.at[r], 1)
+
+        @pl.when(z >= 1 + r)
+        def _():
+            pl.semaphore_wait(from_down.at[r], 1)
+
     q_copies = []
     for o in range(1, depth):
         dest = lax.rem(z + o, depth) * quad + q
         q_copies.append(remote(qbuf.at[0], qbuf.at[o], q_send.at[o], q_recv.at[o], dest))
-    own = remote(cache_hbm, kv.at[1], own_send, own_recv, partner)
 
     row_id = lax.broadcasted_iota(jnp.int32, (drafts, drafts), 0)
     col_id = lax.broadcasted_iota(jnp.int32, (drafts, drafts), 1)
@@ -131,7 +164,7 @@
                 kv.at[2, part], kv.at[3, part], relay_send.at[c], relay_recv.at[c], partner
             ))
 
-    limit = lengths_ref[0]
+    limit = lengths_ref[...]
     joined = rows % 8 == 0 and depth <= 8
     groups = [(0, depth)] if joined else [(o, 1) for o in range(depth)]
     tops = {}
@@ -241,37 +274,70 @@
 
     cols = share_in.shape[2]
     per = 128 // math.gcd(cols, 128)
+    per = per if per % 2 == 0 else 2 * per
+    half = per // 2
     n_groups = n // per
     mine, seat = lax.div(me, per), lax.rem(me, per)
-    get_proj.wait()
+    chip = lax.div(seat, 2)
+    order = list(range(1, n_groups)) + [0]
     share_copies = []
-    for j in list(range(1, n_groups)) + [0]:
+    pair_copies = {}
+    lag = 3
+
+    def project(j):
         target = lax.rem(mine + j, n_groups)
         start = pl.multiple_of(target * (per * cols), 128)
         product = dot_nn(flat, proj[:, pl.ds(start, per * cols)])
         for t in range(per):
             shifted = product if t == 0 else pltpu.roll(product, per * cols - t * cols, 1)
-            share_out[j * per + t] = shifted[:, :cols].astype(jnp.bfloat16)
-        if j > 0:
-            for t in range(per):
-                slot = j * per + seat
+            share[j * per + t] = shifted[:, :cols]
+            pair_out[j * per + t] = shifted[:, :cols].astype(jnp.bfloat16)
+        for u in range(half):
+            slot = j * half + u
+            pair_copies[slot] = remote(
+                pair_out.at[j * per + 2 * u + 1 - core], pair_in.at[slot],
+                pair_send.at[slot], pair_recv.at[slot], partner,
+            )
+
+    def pass_on(j):
+        target = lax.rem(mine + j, n_groups)
+        for u in range(half):
+            slot = j * half + u
+            pair_copies[slot].wait_recv()
+            both = share[j * per + 2 * u + core] + pair_in[slot].astype(jnp.float32)
+            if j > 0:
+                share_out[slot] = both.astype(jnp.bfloat16)
+                place = j * half + chip
                 share_copies.append(remote(
-                    share_out.at[j * per + t], share_in.at[slot],
-                    share_send.at[j * per + t], share_recv.at[slot], target * per + t,
+                    share_out.at[slot], share_in.at[place],
+                    share_send.at[slot], share_recv.at[place], target * per + 2 * u + core,
                 ))
-        else:
-            for s in range(1, per):
-                t = lax.rem(seat + s, per)
+            else:
+                kept[u] = both
+                share_out[slot] = both.astype(jnp.bfloat16)
+        if j == 0:
+            for d in range(1, half):
+                u = lax.rem(chip + d, half)
                 share_copies.append(remote(
-                    share_out.at[t], share_in.at[s],
-                    share_send.at[s], share_recv.at[s], mine * per + t,
+                    share_out.at[u], share_in.at[d],
+                    share_send.at[d], share_recv.at[d], mine * per + 2 * u + core,
                 ))
-    result = share_out[seat].astype(jnp.float32)
-    for s in list(range(1, per)) + list(range(per, n)):
+
+    get_proj.wait()
+    for i, j in enumerate(order):
+        project(j)
+        if i >= lag:
+            pass_on(order[i - lag])
+    for j in order[max(0, n_groups - lag):]:
+        pass_on(j)
+    result = kept[chip]
+    for s in range(1, n // 2):
         arrived(share_in, share_send, share_recv, s).wait_recv()
         result = result + share_in[s].astype(jnp.float32)
     out_ref[...] = result.astype(jnp.bfloat16)
 
+    for copy in pair_copies.values():
+        copy.wait_send()
     own.wait_send()
     for copy in near_copies + relays + q_copies + state_copies + stat_copies + share_copies:
         copy.wait_send()
@@ -287,13 +353,12 @@
     cols = model // n
     anywhere = pl.BlockSpec(memory_space=pl.ANY)
     in_vmem = pl.BlockSpec(memory_space=pltpu.VMEM)
-    in_smem = pl.BlockSpec(memory_space=pltpu.SMEM)
     dma = pltpu.SemaphoreType.DMA
     bf16 = jnp.bfloat16
     return pl.pallas_call(
         functools.partial(kernel, n, quad, heads, drafts, latent, width, vdim),
         out_shape=jax.ShapeDtypeStruct((drafts, cols), bf16),
-        in_specs=[anywhere, anywhere, anywhere, in_smem, in_vmem, anywhere, anywhere],
+        in_specs=[anywhere, anywhere, anywhere, in_vmem, in_vmem, anywhere, anywhere],
         out_specs=in_vmem,
         scratch_shapes=[
             pltpu.VMEM((drafts, heads, width), bf16),
@@ -308,8 +373,14 @@
             pltpu.VMEM((depth, rows, latent), bf16),
             pltpu.VMEM((depth, 8, 128), jnp.float32),
             pltpu.VMEM((depth, 8, 128), jnp.float32),
+            pltpu.VMEM((n, drafts, cols), jnp.float32),
+            pltpu.VMEM((n // 2, drafts, cols), jnp.float32),
             pltpu.VMEM((n, drafts, cols), bf16),
-            pltpu.VMEM((n, drafts, cols), bf16),
+            pltpu.VMEM((n // 2, drafts, cols), bf16),
+            pltpu.VMEM((n // 2, drafts, cols), bf16),
+            pltpu.VMEM((n // 2, drafts, cols), bf16),
+            pltpu.SemaphoreType.REGULAR((depth,)),
+            pltpu.SemaphoreType.REGULAR((depth,)),
             dma((5,)),
             dma, dma,
             dma((pieces,)), dma((pieces,)),
@@ -317,12 +388,13 @@
             dma((depth,)), dma((depth,)),
             dma((depth,)), dma((depth,)),
             dma((depth,)), dma((depth,)),
-            dma((n,)), dma((n,)),
+            dma((n // 2,)), dma((n // 2,)),
+            dma((n // 2,)), dma((n // 2,)),
         ],
         compiler_params=pltpu.CompilerParams(
             collective_id=0, has_side_effects=True, vmem_limit_bytes=56 * 1024 * 1024
         ),
-    )(queries[0], cache[0].T, draft_latent[0], lengths, parents, value_up, out_proj)
+    )(queries[0], cache[0].T, draft_latent[0], lengths.reshape(1, 1), parents, value_up, out_proj)
 
 
 def quad_of(mesh):

time: 45.7 us -> 43.3 us (0.947)
  Pallas kernels: 43.2 us -> 41.1 us
    pallas_call x1, Pallas kernels: 43.2 us -> 41.1 us  [on_device(): pl.pallas_call(functools.partial(kernel, n, quad, heads, drafts, latent,...]
where the time goes in v3:
time: 43.3 us; the launch traced here: 43.1 us
  Pallas kernels  41.1 us (95%)
  local copies, waits for them, and re-layouts  1.35 us (3%)
  between operations  0.66 us (2%)
    pallas_call x1, Pallas kernels, on_device(): pl.pallas_call(functools.partial(kernel, n, quad, heads, drafts, latent,...  41.1 us
    unnamed x1, local copies, waits for them, and re-layouts  1.35 us

profile of v3, /device:TPU:0, one launch (start us, length us, event | category | flops | bytes accessed | tf_op | source)
XLA Modules:
  0.0 43.1 jit_solution(15268967270106058481)
XLA Ops:
  0.7 41.1 %shard_map.73 = bf16[24,448]{1,0:T(8,128)(2,1)} custom-call(bf16[24,4,576]{2,1,0:T(4,128)(2,1)} %bitcast.8, bf16[576,512]{1,0:T(8,128)(2,1)} %bitcast.7, bf16[24,576]{1,0:T(8,128)(2,1)} %bitcast.9, s32[1,1]{1,0:T(1,128)} %bitcast.6.lengths_ref, s32[1,24]{1,0:T(1,128)} %parents_ref.1, bf16[4,512,128]{2,1,0:T(8,128)(2,1)} %up_hbm.1, bf16[512,7168]{1,0:T(8,128)(2,1)} %proj_hbm.1), custom_call_target="tpu_custom_call" | custom-call | tf_op jit(solution)/shard_map/pallas_call | solution.py:358
  41.7 1.3 %copy.10 = bf16[24,448]{1,0:T(8,128)(2,1)} copy(bf16[24,448]{1,0:T(8,128)(2,1)} %shard_map.73) | data formatting | bytes 43008
